TPU v7x, 512 devices: a whole 4x8x8 slice. The times are simulated.
512 devices in a mesh: dp: 4 (over x_lo, core), blk: 128 (over y, z, x_hi).
Axes of the slice: x: 4 (x_hi: 2, x_lo: 2; x = x_hi * 2 + x_lo), y: 8, z: 8, core: 2. Of those that a mesh axis runs over, the one named last changes fastest.
Arguments:
- queries: bfloat16 [4, 24576, 512], P('dp', 'blk'), may hold values from -6 to 6, as said below
- key_in: bfloat16 [4, 24576, 512], P('dp', 'blk'), may hold values from -6 to 6, as said below
- value_in: bfloat16 [4, 24576, 512], P('dp', 'blk'), may hold values from -6 to 6
- out_weight: bfloat16 [512, 1024], replicated, may hold values from -2 to 2
- conv_kernel: float32 [31, 1024], replicated, may hold values from -1 to 1
- cotangent: bfloat16 [4, 24576, 1024], P('dp', 'blk'), may hold values from -6 to 6
Outputs:
- out_frames: bfloat16 [4, 24576, 1024], P('dp', 'blk')
- query_grad: bfloat16 [4, 24576, 512], P('dp', 'blk')
- key_grad: bfloat16 [4, 24576, 512], P('dp', 'blk')
- value_grad: bfloat16 [4, 24576, 512], P('dp', 'blk')
- weight_grad: float32 [512, 1024], replicated
- kernel_grad: float32 [31, 1024], replicated
Inputs may be any that keep to these rules, and one draw needn't show every extreme that they name: `queries`: independent entries. `key_in`: independent entries.
All inputs are finite; a program needn't handle non-finite values.
Results may differ from a plain program's by a relative error of at most 0.024.
Values may be sent and summed in bfloat16 or wider, within the bound.
A program may use at most 64 MiB of HBM per device.

v0:
```python
import math
import jax
import jax.numpy as jnp
from jax import lax
from jax.sharding import PartitionSpec as P

ATT_HEADS = 8
HEAD_DIM = 64
CTX_MAX = 3
ATT = 512
NEGATIVE = -1e30


def from_behind(block, axis, distance):
    devices = range(lax.axis_size(axis))
    route = [(i - distance, i) for i in devices if i - distance in devices]
    return lax.ppermute(block, axis, route)


def split_heads(matrix):
    return matrix.reshape(matrix.shape[0], ATT_HEADS, HEAD_DIM)


def tile_scores(query_heads, tile, query_pos, key_pos, usable, left_span, score_scale):
    key_heads = split_heads(tile[:, :ATT])
    scores = (
        jnp.einsum("qhd,khd->hqk", query_heads, key_heads, preferred_element_type=jnp.float32)
        * score_scale
    )
    distance = query_pos[:, None] - key_pos[None, :]
    visible = ((distance >= 0) & (distance < left_span) & usable)[None]
    return (jnp.where(visible, scores, NEGATIVE), visible)


def attend_tile(
    softmax_state, query_heads, tile, query_pos, key_pos, usable, left_span, score_scale
):
    running_max, running_sum, weighted = softmax_state
    scores, visible = tile_scores(
        query_heads, tile, query_pos, key_pos, usable, left_span, score_scale
    )
    new_max = jnp.maximum(running_max, jnp.max(scores, axis=-1))
    weights = jnp.where(visible, jnp.exp(scores - new_max[..., None]), 0.0)
    fading = jnp.exp(running_max - new_max)
    running_sum = running_sum * fading + jnp.sum(weights, axis=-1)
    value_heads = split_heads(tile[:, ATT:])
    update = jnp.einsum(
        "hqk,khd->qhd",
        weights.astype(jnp.bfloat16),
        value_heads,
        preferred_element_type=jnp.float32,
    )
    weighted = weighted * jnp.transpose(fading)[:, :, None] + update
    return (new_max, running_sum, weighted)


def tile_grads(
    query_heads,
    dout_heads,
    log_sums,
    deltas,
    tile,
    query_pos,
    key_pos,
    usable,
    left_span,
    score_scale,
):
    scores, visible = tile_scores(
        query_heads, tile, query_pos, key_pos, usable, left_span, score_scale
    )
    key_heads = split_heads(tile[:, :ATT])
    value_heads = split_heads(tile[:, ATT:])
    probs = jnp.where(visible, jnp.exp(scores - log_sums[..., None]), 0.0)
    dvalue_heads = jnp.einsum(
        "hqk,qhd->khd", probs.astype(jnp.bfloat16), dout_heads, preferred_element_type=jnp.float32
    )
    dprobs = jnp.einsum("qhd,khd->hqk", dout_heads, value_heads, preferred_element_type=jnp.float32)
    dscores = (probs * (dprobs - deltas[..., None])).astype(jnp.bfloat16)
    dquery = (
        jnp.einsum("hqk,khd->qhd", dscores, key_heads, preferred_element_type=jnp.float32)
        * score_scale
    )
    dkey_heads = (
        jnp.einsum("hqk,qhd->khd", dscores, query_heads, preferred_element_type=jnp.float32)
        * score_scale
    )
    row_count = tile.shape[0]
    return (
        dquery,
        jnp.concatenate(
            [dkey_heads.reshape(row_count, ATT), dvalue_heads.reshape(row_count, ATT)], axis=1
        ),
    )


def depthwise(extended, conv_kernel, row_count, ahead):
    tap_count = conv_kernel.shape[0]

    def add_tap(tap_index, running):
        first_row = tap_index if ahead else tap_count - 1 - tap_index
        return running + conv_kernel[tap_index] * lax.dynamic_slice_in_dim(
            extended, first_row, row_count, 0
        )

    empty = jnp.zeros((row_count, extended.shape[1]), jnp.float32)
    return lax.fori_loop(0, tap_count, add_tap, empty)


def sum_weights(weight_part, kernel_part):
    return lax.psum((weight_part, kernel_part), ("dp", "blk"))


def per_device(queries, key_in, value_in, out_weight, conv_kernel, cotangent):
    cycle_count = lax.axis_size("blk")
    device = lax.axis_index("blk")
    row_count = queries.shape[1]
    context = min(CTX_MAX, cycle_count // 4)
    left_span = context * row_count
    score_scale = 1.0 / math.sqrt(HEAD_DIM)
    edge_rows = conv_kernel.shape[0] - 1
    row_ids = jnp.arange(row_count, dtype=jnp.int32)
    query_heads = split_heads(queries[0])
    own_tile = jnp.concatenate([key_in[0], value_in[0]], axis=1)
    own_pos = device * row_count + row_ids
    always = jnp.array(True)

    def source(offset):
        anchor = device - offset
        return (anchor * row_count + row_ids, anchor >= 0)

    start_state = (
        jnp.full((ATT_HEADS, row_count), NEGATIVE, jnp.float32),
        jnp.zeros((ATT_HEADS, row_count), jnp.float32),
        jnp.zeros((row_count, ATT_HEADS, HEAD_DIM), jnp.float32),
    )
    first_state = attend_tile(
        start_state, query_heads, own_tile, own_pos, own_pos, always, left_span, score_scale
    )

    def forward_step(carry, offset):
        moving, softmax_state = carry
        arrived = from_behind(moving, "blk", 1)
        tile_pos, tile_usable = source(offset)
        softmax_state = attend_tile(
            softmax_state,
            query_heads,
            arrived,
            own_pos,
            tile_pos,
            tile_usable,
            left_span,
            score_scale,
        )
        return ((arrived, softmax_state), arrived)

    offsets = jnp.arange(1, context + 1, dtype=jnp.int32)
    (unused_tile, final_state), kept_tiles = lax.scan(
        forward_step, (own_tile, first_state), offsets
    )
    running_max, running_sum, weighted = final_state
    attended = (weighted / jnp.transpose(running_sum)[:, :, None]).astype(jnp.bfloat16)
    log_sums = running_max + jnp.log(running_sum)
    flat = attended.reshape(row_count, ATT)
    hidden = jnp.dot(flat, out_weight, preferred_element_type=jnp.float32).astype(jnp.bfloat16)
    before = from_behind(hidden[-edge_rows:], "blk", 1)
    extended = jnp.concatenate([before, hidden], axis=0).astype(jnp.float32)
    mixed = depthwise(extended, conv_kernel, row_count, False)
    sigma = jax.nn.sigmoid(mixed)
    out_frames = (mixed * sigma).astype(jnp.bfloat16)[None]
    upstream = cotangent[0].astype(jnp.float32)
    dmixed = upstream * sigma * (1.0 + mixed * (1.0 - sigma))
    after = from_behind(dmixed[:edge_rows].astype(jnp.bfloat16), "blk", -1).astype(jnp.float32)
    dextended = jnp.concatenate([dmixed, after], axis=0)
    dhidden = depthwise(dextended, conv_kernel, row_count, True).astype(jnp.bfloat16)

    def kernel_tap(tap_index):
        window = lax.dynamic_slice_in_dim(extended, edge_rows - tap_index, row_count, 0)
        return jnp.sum(dmixed * window, axis=0)

    kernel_part = lax.map(kernel_tap, jnp.arange(edge_rows + 1, dtype=jnp.int32))
    weight_part = jnp.einsum("ra,rd->ad", flat, dhidden, preferred_element_type=jnp.float32)
    dattended = jnp.einsum(
        "rd,ad->ra", dhidden, out_weight, preferred_element_type=jnp.float32
    ).astype(jnp.bfloat16)
    dout_heads = split_heads(dattended)
    deltas = jnp.einsum("rhe,rhe->hr", dout_heads, attended, preferred_element_type=jnp.float32)
    dquery_own, dkv_own = tile_grads(
        query_heads,
        dout_heads,
        log_sums,
        deltas,
        own_tile,
        own_pos,
        own_pos,
        always,
        left_span,
        score_scale,
    )
    zero_buffer = jnp.zeros((row_count, 2 * ATT), jnp.float32)

    def backward_step(carry, inputs):
        buffer, dquery_sum = carry
        tile, offset = inputs
        tile_pos, tile_usable = source(offset)
        dquery_part, dkv_part = tile_grads(
            query_heads,
            dout_heads,
            log_sums,
            deltas,
            tile,
            own_pos,
            tile_pos,
            tile_usable,
            left_span,
            score_scale,
        )
        arrived = from_behind((buffer + dkv_part).astype(jnp.bfloat16), "blk", -1).astype(
            jnp.float32
        )
        return ((arrived, dquery_sum + dquery_part), None)

    (buffer, dquery_sum), unused = lax.scan(
        backward_step, (zero_buffer, dquery_own), (kept_tiles, offsets), reverse=True
    )
    dkv_total = dkv_own + buffer
    weight_total, kernel_total = sum_weights(weight_part, kernel_part)
    query_grad = dquery_sum.reshape(row_count, ATT).astype(jnp.bfloat16)[None]
    key_grad = dkv_total[:, :ATT].astype(jnp.bfloat16)[None]
    value_grad = dkv_total[:, ATT:].astype(jnp.bfloat16)[None]
    return (out_frames, query_grad, key_grad, value_grad, weight_total, kernel_total)


def solution(mesh):
    return jax.shard_map(
        per_device,
        mesh=mesh,
        in_specs=(
            P("dp", "blk", None),
            P("dp", "blk", None),
            P("dp", "blk", None),
            P(),
            P(),
            P("dp", "blk", None),
        ),
        out_specs=(
            P("dp", "blk", None),
            P("dp", "blk", None),
            P("dp", "blk", None),
            P("dp", "blk", None),
            P(),
            P(),
        ),
        check_vma=False,
    )
```

profile of v0, /device:TPU:24, one launch (start us, length us, event | category | flops | bytes accessed | tf_op | source)
XLA Modules:
  0.0 622.3 jit_solution(3382806898935224929)
XLA Ops:
  12.4 69.9 %while.79 = (s32[]{:T(128)}, bf16[192,1024]{0,1:T(8,128)(2,1)S(1)}, f32[8,192]{1,0:T(8,128)S(1)}, f32[8,192]{1,0:T(8,128)S(1)}, f32[192,8,64]{0,2,1:T(8,128)S(1)...) while((s32[]{:T(128)}, bf16[192,1024]{0,1:T(8,128)(2,1)S(1)}, ...), condition=%wide.region_5.6_spmd.clone, body=%wide.region_2.5_spmd.clone.sunk | while | flops 78537600 | bytes 9227495 | solution.py:158
  12.4 4.9 collective-permute-start
  18.7 18.9 %collective-permute-done = bf16[192,1024]{0,1:T(8,128)(2,1)S(1)} collective-permute-done((bf16[192,1024]{0,1:T(8,128)(2,1)S(1)}, bf16[192,1024]{0,1:T(8,128)(2,1)S(1)}, u32[]{:S(2)}, u32[]{:S(2)}) %collective-permute-start) | collective-permute-done | bytes 393248 | tf_op jit(solution)/shard_map/while/body/eval_jaxpr/ppermute | solution.py:17
  39.8 1.9 collective-permute-start
  43.1 16.2 %collective-permute-done = bf16[192,1024]{0,1:T(8,128)(2,1)S(1)} collective-permute-done((bf16[192,1024]{0,1:T(8,128)(2,1)S(1)}, bf16[192,1024]{0,1:T(8,128)(2,1)S(1)}, u32[]{:S(2)}, u32[]{:S(2)}) %collective-permute-start) | collective-permute-done | bytes 393248 | tf_op jit(solution)/shard_map/while/body/eval_jaxpr/ppermute | solution.py:17
  61.5 1.9 collective-permute-start
  64.8 15.3 %collective-permute-done = bf16[192,1024]{0,1:T(8,128)(2,1)S(1)} collective-permute-done((bf16[192,1024]{0,1:T(8,128)(2,1)S(1)}, bf16[192,1024]{0,1:T(8,128)(2,1)S(1)}, u32[]{:S(2)}, u32[]{:S(2)}) %collective-permute-start) | collective-permute-done | bytes 393248 | tf_op jit(solution)/shard_map/while/body/eval_jaxpr/ppermute | solution.py:17
  82.8 1.9 collective-permute-start.2
  84.9 8.7 %collective-permute-done.2 = bf16[30,1024]{1,0:T(8,128)(2,1)S(1)} collective-permute-done((bf16[30,1024]{1,0:T(8,128)(2,1)S(1)}, bf16[30,1024]{1,0:T(8,128)(2,1)S(1)}, u32[]{:S(2)}, u32[]{:S(2)}) %collective-permute-start.2) | collective-permute-done | bytes 61472 | tf_op jit(solution)/shard_map/ppermute | solution.py:17
  94.6 36.2 %while.80 = (s32[]{:T(128)}, f32[192,1024]{1,0:T(8,128)S(1)}, f32[31,1024]{1,0:T(8,128)}, f32[222,1024]{1,0:T(8,128)S(1)}, s32[]{:T(128)}, /*index=5*/s32[]{:T(128)}, s32[]{:T(128)}, s32[]{:T(128)}) while((s32[]{:T(128)}, f32[192,1024]{1,0:T(8,128)S(1)}, f32[31,1024]{1,0:T(8,128)}, f32[222,1024]{1,0:T(8,128)S(1)}, s32[]{:T(128)}, ...), condition=%wide.region_7.8_spmd.clone, body=%wide.region_6.7_spmd.clone.sunk | while | flops 589831 | bytes 2371741 | solution.py:107
  131.7 2.3 fusion.39
  134.1 1.9 collective-permute-start.3
  136.0 106.3 %while.78 = (s32[]{:T(128)}, f32[31,1024]{1,0:T(8,128)}, s32[31]{0:T(128)S(1)}, f32[222,1024]{1,0:T(8,128)S(1)}, f32[192,1024]{1,0:T(8,128)S(1)}, /*index=5*/s32[]{:T(128)}, s32[1]{0:T(128)}, s32[]{:T(128)}, s32[1]{0:T(128)}) while((s32[]{:T(128)}, f32[31,1024]{1,0:T(8,128)}, s32[31]{0:T(128)S(1)}, f32[222,1024]{1,0:T(8,128)S(1)}, ...), condition=%wide.region_15.16_spmd, body=%wide.region_13.15_spmd.sunk | while | flops 392198 | bytes 1585319 | solution.py:181
  243.8 71.2 %while.81 = (s32[]{:T(128)}, f32[192,1024]{1,0:T(8,128)S(1)}, f32[31,1024]{1,0:T(8,128)}, f32[222,1024]{1,0:T(8,128)}, s32[]{:T(128)}, /*index=5*/s32[]{:T(128)}) while((s32[]{:T(128)}, f32[192,1024]{1,0:T(8,128)S(1)}, f32[31,1024]{1,0:T(8,128)}, f32[222,1024]{1,0:T(8,128)}, s32[]{:T(128)}, /*index=5*/s32[]{:T(128)}) %tuple.190), condition=%wide.region_9.10_spmd.clone, body=%wide.region_8.9_spmd.clone.sunk | while | flops 589827 | bytes 2371679 | solution.py:107
  244.6 1.5 select_add_fusion.5
  246.9 1.5 select_add_fusion.5
  256.1 1.5 select_add_fusion.5
  258.4 1.5 select_add_fusion.5
  315.9 2.4 convolution_convert_fusion.1
  324.2 1.8 fusion.48
  328.3 63.4 %while.82 = (s32[]{:T(128)}, f32[192,1024]{0,1:T(8,128)S(1)}, f32[192,8,64]{0,2,1:T(8,128)}, s32[3]{0:T(128)S(1)}, s32[]{:T(128)}, /*index=5*/bf16[3,192,1024]{1...) while((s32[]{:T(128)}, f32[192,1024]{0,1:T(8,128)S(1)}, ...), condition=%wide.region_11.12_spmd.clone, body=%wide.region_10.11_spmd.clone.sunk | while | flops 192565632 | bytes 15424801 | solution.py:223
  333.5 1.9 collective-permute-start.1
  335.4 2.2 fusion.139
  337.6 10.0 %collective-permute-done.1 = bf16[192,1024]{0,1:T(8,128)(2,1)} collective-permute-done((bf16[192,1024]{0,1:T(8,128)(2,1)}, bf16[192,1024]{0,1:T(8,128)(2,1)}, u32[]{:S(2)}, u32[]{:S(2)}) %collective-permute-start.1) | collective-permute-done | bytes 393248 | tf_op jit(solution)/shard_map/while/body/eval_jaxpr/ppermute | solution.py:17
  354.1 5.3 collective-permute-start.1
  359.4 2.2 fusion.139
  361.6 6.5 %collective-permute-done.1 = bf16[192,1024]{0,1:T(8,128)(2,1)} collective-permute-done((bf16[192,1024]{0,1:T(8,128)(2,1)}, bf16[192,1024]{0,1:T(8,128)(2,1)}, u32[]{:S(2)}, u32[]{:S(2)}) %collective-permute-start.1) | collective-permute-done | bytes 393248 | tf_op jit(solution)/shard_map/while/body/eval_jaxpr/ppermute | solution.py:17
  374.5 8.4 %collective-permute-start.1 = (bf16[192,1024]{0,1:T(8,128)(2,1)}, bf16[192,1024]{0,1:T(8,128)(2,1)}, u32[]{:S(2)}, u32[]{:S(2)}) collective-permute-start(bf16[192,1024]{0,1:T(8,128)(2,1)} %fusion.138), channel_id=1, source_target_pairs={{1,0},{2,1},{3,2},{4,3},{5,4},{6,5},{7,6},{8,7},{9,8},{10,9},{11,1... | collective-permute-start | bytes 1179656 | tf_op jit(solution)/shard_map/while/body/eval_jaxpr/ppermute | solution.py:17
  382.9 2.2 fusion.139
  385.1 5.4 collective-permute-done.1
  395.8 215.8 %all-reduce.3.cloned.1.call-done = (f32[512,1024]{1,0:T(8,128)}, f32[31,1024]{1,0:T(8,128)}) async-done(((f32[512,1024]{1,0:T(8,128)}, f32[31,1024]{1,0:T(8,128)}), (f32[512,1024]{1,0:T(8,128)}, f32[31,1024]{1,0:T(8,128)})) %all-reduce.3.cloned.1.call-update) | async-done | bytes 2224144 | tf_op jit(solution)/shard_map/psum | solution.py:111
  611.6 3.2 copy.121
  (363 shorter events, 214.3 us)
Async XLA Ops:
  7.2 75.2 %copy-start = (bf16[512,1024]{1,0:T(8,128)(2,1)S(1)}, bf16[512,1024]{1,0:T(8,128)(2,1)}, u32[]{:S(2)}) copy-start(bf16[512,1024]{1,0:T(8,128)(2,1)} %param.19) | copy-start | bytes 3145732
  7.2 604.5 %all-reduce.3.cloned.1.call-start = ((), (), s32[]{:S(2)}) async-start(), calls=%async_computation | async-start | bytes 4456448 | tf_op jit(solution)/shard_map/psum | solution.py:111
  8.6 3.1 copy-start.10
  11.3 1.1 copy-start.1
  12.4 25.2 %collective-permute-start = (bf16[192,1024]{0,1:T(8,128)(2,1)S(1)}, bf16[192,1024]{0,1:T(8,128)(2,1)S(1)}, u32[]{:S(2)}, u32[]{:S(2)}) collective-permute-start(bf16[192,1024]{0,1:T(8,128)(2,1)S(1)} %get-tuple-element.1015), channel_id=1, source_target_pairs={{0,1},{1,2},{2,3},{3,4},{4,5},{5,6},{6,7},{7,8},{8,9},{9,10},{10,1... | collective-permute-start | bytes 1179656 | tf_op jit(solution)/shard_map/while/body/eval_jaxpr/ppermute | solution.py:17
  39.8 19.5 %collective-permute-start = (bf16[192,1024]{0,1:T(8,128)(2,1)S(1)}, bf16[192,1024]{0,1:T(8,128)(2,1)S(1)}, u32[]{:S(2)}, u32[]{:S(2)}) collective-permute-start(bf16[192,1024]{0,1:T(8,128)(2,1)S(1)} %get-tuple-element.1015), channel_id=1, source_target_pairs={{0,1},{1,2},{2,3},{3,4},{4,5},{5,6},{6,7},{7,8},{8,9},{9,10},{10,1... | collective-permute-start | bytes 1179656 | tf_op jit(solution)/shard_map/while/body/eval_jaxpr/ppermute | solution.py:17
  61.5 18.6 %collective-permute-start = (bf16[192,1024]{0,1:T(8,128)(2,1)S(1)}, bf16[192,1024]{0,1:T(8,128)(2,1)S(1)}, u32[]{:S(2)}, u32[]{:S(2)}) collective-permute-start(bf16[192,1024]{0,1:T(8,128)(2,1)S(1)} %get-tuple-element.1015), channel_id=1, source_target_pairs={{0,1},{1,2},{2,3},{3,4},{4,5},{5,6},{6,7},{7,8},{8,9},{9,10},{10,1... | collective-permute-start | bytes 1179656 | tf_op jit(solution)/shard_map/while/body/eval_jaxpr/ppermute | solution.py:17
  82.3 2.5 copy-start.7
  82.4 2.5 copy-start.12
  82.8 2.0 copy-start.15
  82.8 10.7 %collective-permute-start.2 = (bf16[30,1024]{1,0:T(8,128)(2,1)S(1)}, bf16[30,1024]{1,0:T(8,128)(2,1)S(1)}, u32[]{:S(2)}, u32[]{:S(2)}) collective-permute-start(bf16[30,1024]{1,0:T(8,128)(2,1)S(1)} %slice.52), channel_id=1, source_target_pairs={{0,1},{1,2},{2,3},{3,4},{4,5},{5,6},{6,7},{7,8},{8,9},{9,10},{10,1... | collective-permute-start | bytes 184328 | tf_op jit(solution)/shard_map/ppermute | solution.py:17
  130.9 0.9 copy-start.8
  134.1 108.3 %collective-permute-start.3 = (bf16[30,1024]{1,0:T(8,128)(2,1)S(1)}, bf16[30,1024]{1,0:T(8,128)(2,1)S(1)}, u32[]{:S(2)}, u32[]{:S(2)}) collective-permute-start(bf16[30,1024]{1,0:T(8,128)(2,1)S(1)} %slice.59), channel_id=1, source_target_pairs={{1,0},{2,1},{3,2},{4,3},{5,4},{6,5},{7,6},{8,7},{9,8},{10,9},{11,1... | collective-permute-start | bytes 184328 | tf_op jit(solution)/shard_map/ppermute | solution.py:17
  242.4 1.5 copy-start.3
  315.0 0.9 copy-start.4
  315.9 4.6 copy-start.2
  321.8 0.9 copy-start.11
  322.7 1.4 copy-start.5
  322.7 1.4 copy-start.13
  324.2 1.8 copy-start.14
  326.9 1.4 copy-start.6
  330.6 0.8 copy-start.9
  333.5 14.1 %collective-permute-start.1 = (bf16[192,1024]{0,1:T(8,128)(2,1)}, bf16[192,1024]{0,1:T(8,128)(2,1)}, u32[]{:S(2)}, u32[]{:S(2)}) collective-permute-start(bf16[192,1024]{0,1:T(8,128)(2,1)} %fusion.138), channel_id=1, source_target_pairs={{1,0},{2,1},{3,2},{4,3},{5,4},{6,5},{7,6},{8,7},{9,8},{10,9},{11,1... | collective-permute-start | bytes 1179656 | tf_op jit(solution)/shard_map/while/body/eval_jaxpr/ppermute | solution.py:17
  351.2 0.8 copy-start.9
  354.1 14.0 %collective-permute-start.1 = (bf16[192,1024]{0,1:T(8,128)(2,1)}, bf16[192,1024]{0,1:T(8,128)(2,1)}, u32[]{:S(2)}, u32[]{:S(2)}) collective-permute-start(bf16[192,1024]{0,1:T(8,128)(2,1)} %fusion.138), channel_id=1, source_target_pairs={{1,0},{2,1},{3,2},{4,3},{5,4},{6,5},{7,6},{8,7},{9,8},{10,9},{11,1... | collective-permute-start | bytes 1179656 | tf_op jit(solution)/shard_map/while/body/eval_jaxpr/ppermute | solution.py:17
  371.6 0.8 copy-start.9
  374.5 16.0 %collective-permute-start.1 = (bf16[192,1024]{0,1:T(8,128)(2,1)}, bf16[192,1024]{0,1:T(8,128)(2,1)}, u32[]{:S(2)}, u32[]{:S(2)}) collective-permute-start(bf16[192,1024]{0,1:T(8,128)(2,1)} %fusion.138), channel_id=1, source_target_pairs={{1,0},{2,1},{3,2},{4,3},{5,4},{6,5},{7,6},{8,7},{9,8},{10,9},{11,1... | collective-permute-start | bytes 1179656 | tf_op jit(solution)/shard_map/while/body/eval_jaxpr/ppermute | solution.py:17
  611.6 3.2 copy-start.16
Sparse Core Ops, SparseCore 0:
  328.0 283.6 all-reduce.2
where the time goes:
time: 632 us; the launch traced here: 622 us
  waiting for transfers between devices  297 us (47%)
  local copies, waits for them, and re-layouts  134 us (21%)
  other arithmetic  79.2 us (13%)
  loops' own time  46.3 us (7%)
  starting transfers between devices  28.2 us (4%)
  matrix products  23.3 us (4%)
  between operations  14.4 us (2%)
    psum x1, waiting for transfers between devices, sum_weights(): return lax.psum((weight_part, kernel_part), ('dp', 'blk'))  216 us
    ppermute x8, waiting for transfers between devices, from_behind(): return lax.ppermute(block, axis, route)  81.1 us
    add x62, other arithmetic, add_tap(): running + conv_kernel[tap_index] * lax.dynamic_slice_in_dim(extended, fir...  58.3 us
    dynamic_slice x62, local copies, waits for them, and re-layouts, add_tap(): conv_kernel[tap_index]  47.7 us
    dynamic_update_slice x31, local copies, waits for them, and re-layouts, per_device(): lax.map(kernel_tap, jnp.arange(edge_rows + 1, dtype=jnp.int32))  43.4 us
    another operation x1, loops' own time, per_device(): lax.map(kernel_tap, jnp.arange(edge_rows + 1, dtype=jnp.int32))  40.4 us
    ppermute x8, starting transfers between devices, from_behind(): return lax.ppermute(block, axis, route)  28.1 us
    dynamic_slice x31, local copies, waits for them, and re-layouts, per_device(): lax.map(kernel_tap, jnp.arange(edge_rows + 1, dtype=jnp.int32))  18 us
  transfers between devices with their start and end apart: 9, of which 8 were waited for; matrix products, arithmetic and copies ran while one was open for 15% of the time, Pallas kernels for 0%

commit v1 on v0

--- a/solution.py
+++ b/solution.py
@@ -108,7 +108,7 @@
 
 
 def sum_weights(weight_part, kernel_part):
-    return lax.psum((weight_part, kernel_part), ("dp", "blk"))
+    return lax.psum(lax.psum((weight_part, kernel_part), "blk"), "dp")
 
 
 def per_device(queries, key_in, value_in, out_weight, conv_kernel, cotangent):

time: 632 us -> 1740 us (2.75)
  the two profiles are of different devices: /device:TPU:24 before, /device:TPU:11 now
where the time goes in v1:
time: 1740 us
  waiting for transfers between devices  1410 us (81%)
  local copies, waits for them, and re-layouts  134 us (8%)
  other arithmetic  79.1 us (5%)
  loops' own time  46.3 us (3%)
  starting transfers between devices  30.2 us (2%)
  matrix products  24.4 us (1%)
    psum x2, waiting for transfers between devices, sum_weights(): return lax.psum(lax.psum((weight_part, kernel_part), 'blk'), 'dp')  1340 us
    ppermute x8, waiting for transfers between devices, from_behind(): return lax.ppermute(block, axis, route)  70.9 us
    add x62, other arithmetic, add_tap(): running + conv_kernel[tap_index] * lax.dynamic_slice_in_dim(extended, fir...  58.3 us
    dynamic_slice x62, local copies, waits for them, and re-layouts, add_tap(): conv_kernel[tap_index]  47.7 us
    dynamic_update_slice x31, local copies, waits for them, and re-layouts, per_device(): lax.map(kernel_tap, jnp.arange(edge_rows + 1, dtype=jnp.int32))  43.4 us
    another operation x1, loops' own time, per_device(): lax.map(kernel_tap, jnp.arange(edge_rows + 1, dtype=jnp.int32))  40.4 us
  transfers between devices with their start and end apart: 10, of which 9 were waited for; matrix products, arithmetic and copies ran while one was open for 6% of the time, Pallas kernels for 0%

profile of v1, /device:TPU:11, one launch (start us, length us, event | category | flops | bytes accessed | tf_op | source)
XLA Modules:
  0.0 1735.5 jit_solution(4325754507855716979)
XLA Ops:
  12.4 66.6 %while.79 = (s32[]{:T(128)}, bf16[192,1024]{0,1:T(8,128)(2,1)S(1)}, f32[8,192]{1,0:T(8,128)S(1)}, f32[8,192]{1,0:T(8,128)S(1)}, f32[192,8,64]{0,2,1:T(8,128)S(1)...) while((s32[]{:T(128)}, bf16[192,1024]{0,1:T(8,128)(2,1)S(1)}, ...), condition=%wide.region_5.6_spmd.clone, body=%wide.region_2.5_spmd.clone.sunk | while | flops 78537600 | bytes 9227495 | solution.py:158
  12.4 3.7 collective-permute-start
  17.5 18.6 %collective-permute-done = bf16[192,1024]{0,1:T(8,128)(2,1)S(1)} collective-permute-done((bf16[192,1024]{0,1:T(8,128)(2,1)S(1)}, bf16[192,1024]{0,1:T(8,128)(2,1)S(1)}, u32[]{:S(2)}, u32[]{:S(2)}) %collective-permute-start) | collective-permute-done | bytes 393248 | tf_op jit(solution)/shard_map/while/body/eval_jaxpr/ppermute | solution.py:17
  38.3 1.9 collective-permute-start
  41.6 15.3 collective-permute-done
  59.1 1.9 collective-permute-start
  62.4 14.3 collective-permute-done
  79.5 1.9 collective-permute-start.2
  81.5 7.5 collective-permute-done.2
  90.1 36.2 %while.80 = (s32[]{:T(128)}, f32[192,1024]{1,0:T(8,128)S(1)}, f32[31,1024]{1,0:T(8,128)}, f32[222,1024]{1,0:T(8,128)S(1)}, s32[]{:T(128)}, /*index=5*/s32[]{:T(128)}, s32[]{:T(128)}, s32[]{:T(128)}) while((s32[]{:T(128)}, f32[192,1024]{1,0:T(8,128)S(1)}, f32[31,1024]{1,0:T(8,128)}, f32[222,1024]{1,0:T(8,128)S(1)}, s32[]{:T(128)}, ...), condition=%wide.region_7.8_spmd.clone, body=%wide.region_6.7_spmd.clone.sunk | while | flops 589831 | bytes 2371741 | solution.py:107
  127.2 2.3 fusion.39
  129.6 1.9 collective-permute-start.3
  131.5 106.3 %while.78 = (s32[]{:T(128)}, f32[31,1024]{1,0:T(8,128)}, s32[31]{0:T(128)S(1)}, f32[222,1024]{1,0:T(8,128)S(1)}, f32[192,1024]{1,0:T(8,128)S(1)}, /*index=5*/s32[]{:T(128)}, s32[1]{0:T(128)}, s32[]{:T(128)}, s32[1]{0:T(128)}) while((s32[]{:T(128)}, f32[31,1024]{1,0:T(8,128)}, s32[31]{0:T(128)S(1)}, f32[222,1024]{1,0:T(8,128)S(1)}, ...), condition=%wide.region_16.17_spmd, body=%wide.region_14.16_spmd.sunk | while | flops 392198 | bytes 1585319 | solution.py:181
  239.3 71.2 %while.81 = (s32[]{:T(128)}, f32[192,1024]{1,0:T(8,128)S(1)}, f32[31,1024]{1,0:T(8,128)}, f32[222,1024]{1,0:T(8,128)}, s32[]{:T(128)}, /*index=5*/s32[]{:T(128)}) while((s32[]{:T(128)}, f32[192,1024]{1,0:T(8,128)S(1)}, f32[31,1024]{1,0:T(8,128)}, f32[222,1024]{1,0:T(8,128)}, s32[]{:T(128)}, /*index=5*/s32[]{:T(128)}) %tuple.193), condition=%wide.region_9.10_spmd.clone, body=%wide.region_8.9_spmd.clone.sunk | while | flops 589827 | bytes 2371679 | solution.py:107
  240.1 1.5 select_add_fusion.5
  310.5 1.8 fusion.48
  312.4 2.4 convolution_convert_fusion.1
  317.1 2.0 copy.51
  323.0 2.3 fusion.33
  325.3 1236.3 %all-reduce.5.cloned.1.call-done = (f32[512,1024]{1,0:T(8,128)}, f32[31,1024]{1,0:T(8,128)}) async-done(((f32[512,1024]{1,0:T(8,128)}, f32[31,1024]{1,0:T(8,128)}), (f32[512,1024]{1,0:T(8,128)}, f32[31,1024]{1,0:T(8,128)})) %all-reduce.5.cloned.1.call-update) | async-done | bytes 2224144 | tf_op jit(solution)/shard_map/psum | solution.py:111
  1561.7 59.7 %while.82 = (s32[]{:T(128)}, f32[192,1024]{0,1:T(8,128)S(1)}, f32[192,8,64]{0,2,1:T(8,128)}, s32[3]{0:T(128)S(1)}, s32[]{:T(128)}, /*index=5*/bf16[3,192,1024]{1...) while((s32[]{:T(128)}, f32[192,1024]{0,1:T(8,128)S(1)}, ...), condition=%wide.region_11.12_spmd.clone, body=%wide.region_10.11_spmd.clone.sunk | while | flops 192565632 | bytes 15424801 | solution.py:223
  1567.0 3.9 collective-permute-start.1
  1570.8 2.2 fusion.139
  1573.0 6.3 collective-permute-done.1
  1585.7 6.5 collective-permute-start.1
  1592.3 2.2 fusion.139
  1594.5 4.5 collective-permute-done.1
  1605.3 8.4 collective-permute-start.1
  1613.7 2.2 fusion.139
  1615.9 4.3 collective-permute-done.1
  1625.6 99.2 %all-reduce.7.cloned.1.call-done = (f32[512,1024]{1,0:T(8,128)}, f32[31,1024]{1,0:T(8,128)}) async-done(((f32[512,1024]{1,0:T(8,128)}, f32[31,1024]{1,0:T(8,128)}), (f32[512,1024]{1,0:T(8,128)}, f32[31,1024]{1,0:T(8,128)})) %all-reduce.7.cloned.1.call-update) | async-done | bytes 2224144 | tf_op jit(solution)/shard_map/psum | solution.py:111
  1724.8 3.2 copy.123
  (364 shorter events, 216.1 us)
Async XLA Ops:
  7.2 71.9 %copy-start = (bf16[512,1024]{1,0:T(8,128)(2,1)S(1)}, bf16[512,1024]{1,0:T(8,128)(2,1)}, u32[]{:S(2)}) copy-start(bf16[512,1024]{1,0:T(8,128)(2,1)} %param.19) | copy-start | bytes 3145732
  7.2 1554.4 %all-reduce.5.cloned.1.call-start = ((), (), s32[]{:S(2)}) async-start(), calls=%async_computation | async-start | bytes 4456448 | tf_op jit(solution)/shard_map/psum | solution.py:111
  8.6 3.1 copy-start.10
  11.3 1.1 copy-start.1
  12.4 23.7 %collective-permute-start = (bf16[192,1024]{0,1:T(8,128)(2,1)S(1)}, bf16[192,1024]{0,1:T(8,128)(2,1)S(1)}, u32[]{:S(2)}, u32[]{:S(2)}) collective-permute-start(bf16[192,1024]{0,1:T(8,128)(2,1)S(1)} %get-tuple-element.1017), channel_id=1, source_target_pairs={{0,1},{1,2},{2,3},{3,4},{4,5},{5,6},{6,7},{7,8},{8,9},{9,10},{10,1... | collective-permute-start | bytes 1179656 | tf_op jit(solution)/shard_map/while/body/eval_jaxpr/ppermute | solution.py:17
  38.3 18.6 %collective-permute-start = (bf16[192,1024]{0,1:T(8,128)(2,1)S(1)}, bf16[192,1024]{0,1:T(8,128)(2,1)S(1)}, u32[]{:S(2)}, u32[]{:S(2)}) collective-permute-start(bf16[192,1024]{0,1:T(8,128)(2,1)S(1)} %get-tuple-element.1017), channel_id=1, source_target_pairs={{0,1},{1,2},{2,3},{3,4},{4,5},{5,6},{6,7},{7,8},{8,9},{9,10},{10,1... | collective-permute-start | bytes 1179656 | tf_op jit(solution)/shard_map/while/body/eval_jaxpr/ppermute | solution.py:17
  59.1 17.6 %collective-permute-start = (bf16[192,1024]{0,1:T(8,128)(2,1)S(1)}, bf16[192,1024]{0,1:T(8,128)(2,1)S(1)}, u32[]{:S(2)}, u32[]{:S(2)}) collective-permute-start(bf16[192,1024]{0,1:T(8,128)(2,1)S(1)} %get-tuple-element.1017), channel_id=1, source_target_pairs={{0,1},{1,2},{2,3},{3,4},{4,5},{5,6},{6,7},{7,8},{8,9},{9,10},{10,1... | collective-permute-start | bytes 1179656 | tf_op jit(solution)/shard_map/while/body/eval_jaxpr/ppermute | solution.py:17
  79.0 2.5 copy-start.6
  79.0 2.4 copy-start.12
  79.5 2.0 copy-start.14
  79.5 9.5 collective-permute-start.2
  126.4 0.9 copy-start.7
  129.6 108.2 %collective-permute-start.3 = (bf16[30,1024]{1,0:T(8,128)(2,1)S(1)}, bf16[30,1024]{1,0:T(8,128)(2,1)S(1)}, u32[]{:S(2)}, u32[]{:S(2)}) collective-permute-start(bf16[30,1024]{1,0:T(8,128)(2,1)S(1)} %slice.59), channel_id=1, source_target_pairs={{1,0},{2,1},{3,2},{4,3},{5,4},{6,5},{7,6},{8,7},{9,8},{10,9},{11,1... | collective-permute-start | bytes 184328 | tf_op jit(solution)/shard_map/ppermute | solution.py:17
  237.8 1.5 copy-start.3
  239.3 71.2 %copy-start.13 = (bf16[192,8,64]{0,2,1:T(8,128)(2,1)S(1)}, bf16[192,8,64]{0,2,1:T(8,128)(2,1)}, u32[]{:S(2)}) copy-start(bf16[192,8,64]{0,2,1:T(8,128)(2,1)} %copy-done.12) | copy-start | bytes 589828
  310.5 1.8 copy-start.4
  312.3 3.6 copy-start.2
  312.3 1412.5 %all-reduce.7.cloned.1.call-start = ((), (), s32[]{:S(2)}) async-start(), calls=%async_computation.1 | async-start | bytes 4456448 | tf_op jit(solution)/shard_map/psum | solution.py:111
  320.8 0.9 copy-start.9
  321.7 1.4 copy-start.11
  323.0 1238.6 %copy-start.5 = (f32[192,1024]{0,1:T(8,128)S(1)}, f32[192,1024]{0,1:T(8,128)}, u32[]{:S(2)}) copy-start(f32[192,1024]{0,1:T(8,128)} %custom-call.2) | copy-start | bytes 2359300
  1564.0 0.8 copy-start.8
  1567.0 12.4 collective-permute-start.1
  1582.8 0.8 copy-start.8
  1585.7 13.2 collective-permute-start.1
  1602.4 0.8 copy-start.8
  1605.3 15.0 collective-permute-start.1
  1724.8 3.2 copy-start.15
Sparse Core Ops, SparseCore 0:
  312.4 1249.1 all-reduce.4
  1565.0 159.7 all-reduce.6
